TPU v7x, 32 devices: a whole 2x2x4 slice. The times are simulated.
32 devices in a mesh: ctx: 8 (over z, x), ch: 4 (over y, core).
Axes of the slice: x: 2, y: 2, z: 4, core: 2. Of those that a mesh axis runs over, the one named last changes fastest.
Arguments:
- signal: float32 [64, 65536], P('ch', 'ctx'), parts along dimension 0, may hold values from -6 to 6
- gate: float32 [64, 65536], P('ch', 'ctx'), parts along dimension 0, may hold values from -6 to 6
- skip: float32 [64], P('ch'), parts along dimension 0, may hold values from 0.5 to 1.5
- filter_spectrum: float32 [16, 2, 64, 8192], P('ctx', None, 'ch'), parts along dimension 2, may hold values from -6 to 6
Outputs:
- gated: float32 [64, 65536], P('ch', 'ctx'), parts along dimension 0
There are 4 independent parts, one for each index of `ch`. A program takes and returns all parts, laid end to end along the dimension named above; each array names one. Nothing has to cross between parts.
All inputs are finite; a program needn't handle non-finite values.
Results may differ from a plain program's by a relative error of at most 0.00005.
Values sent between devices are 32-bit elements; how exact they have to be, the bound alone decides.
No kernel may reach another device: no remote copies, remote signals or barrier semaphores. Data moves between devices by JAX's collectives and lax.ppermute only.
A program may use at most 128 MiB of HBM per device.

v0:
```python
import math
import jax
import jax.numpy as jnp
from jax import lax
from jax.sharding import PartitionSpec as P


def contract(form, left, right):
    return jnp.einsum(form, left, right, precision=lax.Precision.HIGHEST)


def phase_table(left, right, period):
    angle = left * right % period
    theta = angle.astype(jnp.float32) * (2.0 * math.pi / period)
    return (jnp.cos(theta), jnp.sin(theta))


def product_pair(form, left, right):
    real_part = contract(form, left[0], right[0]) - contract(form, left[1], right[1])
    imag_part = contract(form, left[0], right[1]) + contract(form, left[1], right[0])
    return (real_part, imag_part)


def times_pair(left, right):
    return (left[0] * right[0] - left[1] * right[1], left[0] * right[1] + left[1] * right[0])


def local_tables(length):
    outer_len = 128
    inner_len = length // outer_len
    outer_index = jnp.arange(outer_len, dtype=jnp.int32)
    inner_index = jnp.arange(inner_len, dtype=jnp.int32)
    outer_wave = phase_table(outer_index[:, None], outer_index[None, :], outer_len)
    twist_wave = phase_table(outer_index[:, None], inner_index[None, :], length)
    inner_wave = phase_table(inner_index[:, None], inner_index[None, :], inner_len)
    return (outer_len, inner_len, outer_wave, twist_wave, inner_wave)


def local_forward(values, length):
    outer_len, inner_len, outer_wave, twist_wave, inner_wave = local_tables(length)
    lead_shape = values[0].shape[:-1]
    values = tuple((part.reshape(lead_shape + (outer_len, inner_len)) for part in values))
    values = product_pair("as,...sb->...ab", (outer_wave[0], -outer_wave[1]), values)
    values = times_pair(values, (twist_wave[0], -twist_wave[1]))
    return product_pair("...as,bs->...ab", values, (inner_wave[0], -inner_wave[1]))


def local_inverse(values, length):
    outer_len, inner_len, outer_wave, twist_wave, inner_wave = local_tables(length)
    lead_shape = values[0].shape[:-2]
    values = product_pair("...ak,sk->...as", values, inner_wave)
    values = times_pair(values, twist_wave)
    values = product_pair("ta,...as->...ts", outer_wave, values)
    return tuple((part.reshape(lead_shape + (length,)) for part in values))


def shards(signal, gate, skip, filter_spectrum):
    parts_count = lax.axis_size("ctx")
    freq_rows = 2 * parts_count
    channels, tok_local = signal.shape
    slice_len = tok_local // parts_count
    full_len = freq_rows * tok_local
    device = lax.axis_index("ctx")
    is_first = device == 0
    columns = lax.all_to_all(signal[None], "ctx", split_axis=2, concat_axis=0, tiled=True)
    source_row = jnp.arange(parts_count, dtype=jnp.int32)
    dest_index = jnp.arange(parts_count, dtype=jnp.int32)
    slice_pos = device * slice_len + jnp.arange(slice_len, dtype=jnp.int32)
    upper_freq = jnp.where(dest_index == 0, parts_count, freq_rows - dest_index)
    row_freq = jnp.stack([dest_index, upper_freq], axis=1).reshape(freq_rows)
    spot = jnp.arange(tok_local, dtype=jnp.int32)
    wave_cos, wave_sin = phase_table(row_freq[:, None], source_row[None, :], freq_rows)
    first_re = contract("kr,rcq->kcq", wave_cos, columns)
    first_im = -contract("kr,rcq->kcq", wave_sin, columns)
    twist_cos, twist_sin = phase_table(row_freq[:, None], slice_pos[None, :], full_len)
    first_pair = times_pair((first_re, first_im), (twist_cos[:, None, :], -twist_sin[:, None, :]))
    stacked = jnp.stack(first_pair, axis=1)
    moved = lax.all_to_all(stacked, "ctx", split_axis=0, concat_axis=3, tiled=True)
    low_pair = (moved[0, 0], moved[0, 1])
    high_pair = (moved[1, 0], moved[1, 1])
    rows_pair = (jnp.stack([low_pair[0], high_pair[0]]), jnp.stack([low_pair[1], high_pair[1]]))
    spectral = local_forward(rows_pair, tok_local)
    inner_len = tok_local // 128
    filt = filter_spectrum.reshape(2, 2, channels, inner_len, 128).swapaxes(3, 4)
    product = times_pair(spectral, (filt[:, 0], filt[:, 1]))
    restored = local_inverse(product, tok_local)
    my_freq = jnp.stack([device, jnp.where(is_first, parts_count, freq_rows - device)])
    back_cos, back_sin = phase_table(my_freq[:, None], spot[None, :], full_len)
    turned = times_pair(restored, (back_cos[:, None, :], back_sin[:, None, :]))
    scale_factor = 1.0 / full_len
    stacked = jnp.stack(turned, axis=1)
    moved = lax.all_to_all(stacked, "ctx", split_axis=3, concat_axis=0, tiled=True)
    out_cos, out_sin = phase_table(source_row[:, None], row_freq[None, :], freq_rows)
    rows_all = contract("rm,mcq->rcq", out_cos, moved[:, 0]) - contract(
        "rm,mcq->rcq", out_sin, moved[:, 1]
    )
    rows_all = rows_all * scale_factor
    convolved = lax.all_to_all(rows_all, "ctx", split_axis=0, concat_axis=2, tiled=True)
    return gate * (convolved[0] + skip[:, None] * signal)


def solution(mesh):
    return jax.shard_map(
        shards,
        mesh=mesh,
        in_specs=(P("ch", "ctx"), P("ch", "ctx"), P("ch"), P("ctx", None, "ch", None)),
        out_specs=P("ch", "ctx"),
        check_vma=False,
    )
```

profile of v0, /device:TPU:0, one launch (start us, length us, event | category | flops | bytes accessed | tf_op | source)
XLA Modules:
  0.0 351.3 jit_solution(4517637440117171831)
XLA Ops:
  0.0 3.5 copy.33
  4.0 38.3 %reduce = f32[8192,16]{1,0:T(8,128)} reduce(f32[8192,1,16]{2,1,0:T(1,128)} %bitcast.158, f32[]{:T(128)} %broadcast.483), dimensions={1}, to_apply=%bitcast.139.reduce_sub_computation | reduce | bytes 1048580
  42.3 4.4 %reshape.260 = f32[8,1,16384]{2,1,0:T(1,128)} reshape(f32[8192,16]{1,0:T(8,128)} %reduce) | data formatting | bytes 1048576
  46.7 7.8 %all-to-all-start = ((f32[8,1,16384]{2,1,0:T(1,128)}), f32[8,1,16384]{2,1,0:T(1,128)S(1)}, u32[]{:S(2)}, u32[]{:S(2)}) async-start(f32[8,1,16384]{2,1,0:T(1,128)} %reshape.260), calls=%async_computation | async-start | bytes 1048576 | tf_op jit(solution)/shard_map/all_to_all | solution.py:65
  55.1 13.9 %all-to-all-done = f32[8,1,16384]{2,1,0:T(1,128)S(1)} async-done(((f32[8,1,16384]{2,1,0:T(1,128)}), f32[8,1,16384]{2,1,0:T(1,128)S(1)}, u32[]{:S(2)}, u32[]{:S(2)}) %all-to-all-start) | async-done | bytes 524320 | tf_op jit(solution)/shard_map/all_to_all | solution.py:65
  70.7 10.2 %reshape.261 = f32[8192,1,16]{2,1,0:T(1,128)} reshape(f32[8,16384]{1,0:T(8,128)S(1)} %reduce.1) | data formatting | bytes 1048576
  80.9 2.9 copy.55
  86.4 2.5 copy.35
  89.0 3.6 %all-to-all-start.1 = ((f32[16,2,16,1024]{3,2,1,0:T(8,128)}), f32[16,2,16,1024]{3,2,1,0:T(8,128)S(1)}, u32[]{:S(2)}, u32[]{:S(2)}) async-start(f32[16,2,16,1024]{3,2,1,0:T(8,128)} %copy.35), calls=%async_computation.1 | async-start | bytes 4194304 | tf_op jit(solution)/shard_map/all_to_all | solution.py:78
  97.7 43.4 %all-to-all-done.1 = f32[16,2,16,1024]{3,2,1,0:T(8,128)S(1)} async-done(((f32[16,2,16,1024]{3,2,1,0:T(8,128)}), f32[16,2,16,1024]{3,2,1,0:T(8,128)S(1)}, u32[]{:S(2)}, u32[]{:S(2)}) %all-to-all-start.1) | async-done | bytes 2097184 | tf_op jit(solution)/shard_map/all_to_all | solution.py:78
  141.0 2.5 copy.64
  160.9 2.1 multiply_add_fusion.2
  169.0 2.2 fusion.13
  174.4 2.1 reshape.248
  176.5 3.5 fusion.1
  185.1 15.4 %copy.44 = f32[2,2,16,8192]{2,0,1,3:T(2,128)} copy(f32[2,2,16,8192]{3,2,0,1:T(8,128)S(1)} %pad_maximum_fusion.1) | data formatting | bytes 4194304 | tf_op jit(solution)/shard_map/stack | solution.py:91
  200.4 24.0 %reshape.262 = f32[8,1,65536]{2,1,0:T(1,128)S(1)} reshape(f32[8192,2,2,16]{3,2,1,0:T(2,128)} %bitcast.155) | data formatting | bytes 4194304
  224.5 51.9 %all_to_all.69 = f32[8,1,65536]{2,1,0:T(1,128)} all-to-all(f32[8,1,65536]{2,1,0:T(1,128)S(1)} %reshape.262), channel_id=1, replica_groups=mesh['ctx'=8,'ch'=4] {'ctx'}, dimensions={0} | all-to-all | bytes 4194304 | tf_op jit(solution)/shard_map/all_to_all | solution.py:92
  276.4 7.1 %reduce.2 = f32[8,65536]{1,0:T(8,128)S(1)} reduce(f32[8,1,65536]{2,1,0:T(1,128)} %all_to_all.69, f32[]{:T(128)} %broadcast.483), dimensions={1}, to_apply=%all_to_all.58.reduce_sub_computation | reduce | bytes 4194308 | tf_op jit(solution)/shard_map/all_to_all | solution.py:92
  283.5 28.4 %reshape.263 = f32[8192,2,2,16]{3,2,1,0:T(2,128)} reshape(f32[8,65536]{1,0:T(8,128)S(1)} %reduce.2) | data formatting | bytes 4194304
  312.0 13.2 %copy.57 = f32[2,2,16,8,1024]{4,3,2,1,0:T(8,128)S(1)} copy(f32[2,2,16,8,1024]{2,0,1,4,3:T(2,128)} %bitcast.156) | data formatting | bytes 4194304 | tf_op jit(solution)/shard_map/all_to_all | solution.py:92
  325.2 3.0 copy.46
  328.2 2.7 all_to_all.61
  332.5 17.6 %all_to_all.70 = f32[8,16,1024]{2,1,0:T(8,128)S(1)} all-to-all(f32[8,16,1024]{2,1,0:T(8,128)S(1)} %copy.47), channel_id=1, replica_groups=mesh['ctx'=8,'ch'=4] {'ctx'}, dimensions={0} | all-to-all | bytes 1048576 | tf_op jit(solution)/shard_map/all_to_all | solution.py:98
  (59 shorter events, 44.4 us)
Async XLA Ops:
  46.7 22.2 %all-to-all-start = ((f32[8,1,16384]{2,1,0:T(1,128)}), f32[8,1,16384]{2,1,0:T(1,128)S(1)}, u32[]{:S(2)}, u32[]{:S(2)}) async-start(f32[8,1,16384]{2,1,0:T(1,128)} %reshape.260), calls=%async_computation | async-start | bytes 1048576 | tf_op jit(solution)/shard_map/all_to_all | solution.py:65
  89.0 52.1 %all-to-all-start.1 = ((f32[16,2,16,1024]{3,2,1,0:T(8,128)}), f32[16,2,16,1024]{3,2,1,0:T(8,128)S(1)}, u32[]{:S(2)}, u32[]{:S(2)}) async-start(f32[16,2,16,1024]{3,2,1,0:T(8,128)} %copy.35), calls=%async_computation.1 | async-start | bytes 4194304 | tf_op jit(solution)/shard_map/all_to_all | solution.py:78
  159.3 1.6 copy-start
  332.2 18.0 %copy-start.1 = (f32[16,8192]{1,0:T(8,128)S(1)}, f32[16,8192]{1,0:T(8,128)}, u32[]{:S(2)}) copy-start(f32[16,8192]{1,0:T(8,128)} %param.4) | copy-start | bytes 1572868
  332.2 18.0 %copy-start.2 = (f32[16,8192]{1,0:T(8,128)S(1)}, f32[16,8192]{1,0:T(8,128)}, u32[]{:S(2)}) copy-start(f32[16,8192]{1,0:T(8,128)} %param.5) | copy-start | bytes 1572868
  332.2 18.0 %copy-start.3 = (f32[16]{0:T(128)S(1)}, f32[16]{0:T(128)}, u32[]{:S(2)}) copy-start(f32[16]{0:T(128)} %param.6) | copy-start | bytes 196
where the time goes:
time: 357 us; the launch traced here: 351 us
  local copies, waits for them, and re-layouts  133 us (37%)
  blocking collectives  69.5 us (19%)
  waiting for transfers between devices  57.2 us (16%)
  other arithmetic  52 us (15%)
  matrix products  27.5 us (8%)
  starting transfers between devices  11.4 us (3%)
    unnamed x16, local copies, waits for them, and re-layouts  73.3 us
    all_to_all x1, blocking collectives, shards(): lax.all_to_all(stacked, 'ctx', split_axis=3, concat_axis=0, tiled=True)  51.9 us
    all_to_all x1, waiting for transfers between devices, shards(): lax.all_to_all(stacked, 'ctx', split_axis=0, concat_axis=3, tiled=True)  43.4 us
    unnamed x1, other arithmetic  38.3 us
    dot_general x20, matrix products, contract(): return jnp.einsum(form, left, right, precision=lax.Precision.HIGHEST)  27.5 us
    all_to_all x3, local copies, waits for them, and re-layouts, shards(): lax.all_to_all(stacked, 'ctx', split_axis=3, concat_axis=0, tiled=True)  18.9 us
    all_to_all x1, blocking collectives, shards(): lax.all_to_all(rows_all, 'ctx', split_axis=0, concat_axis=2, tiled=True)  17.6 us
    another operation x1, local copies, waits for them, and re-layouts, shards(): stacked = jnp.stack(turned, axis=1)  15.4 us
  transfers between devices with their start and end apart: 2, of which 2 were waited for; matrix products, arithmetic and copies ran while one was open for 2% of the time, Pallas kernels for 0%

commit v1 on v0

--- a/solution.py
+++ b/solution.py
@@ -3,6 +3,22 @@
 import jax.numpy as jnp
 from jax import lax
 from jax.sharding import PartitionSpec as P
+
+
+def pairwise_exchange(x, axis, split, join):
+    ways, here = (lax.axis_size(axis), lax.axis_index(axis))
+    width = x.shape[split] // ways
+    shape = list(x.shape)
+    shape[split] = width
+    height = shape[join]
+    shape[join] = height * ways
+    full = jnp.zeros(shape, x.dtype)
+    for mask in range(ways):
+        part = lax.dynamic_slice_in_dim(x, (here ^ mask) * width, width, axis=split)
+        if mask:
+            part = lax.ppermute(part, axis, [(d, d ^ mask) for d in range(ways)])
+        full = lax.dynamic_update_slice_in_dim(full, part, (here ^ mask) * height, axis=join)
+    return full
 
 
 def contract(form, left, right):
@@ -75,7 +91,7 @@
     twist_cos, twist_sin = phase_table(row_freq[:, None], slice_pos[None, :], full_len)
     first_pair = times_pair((first_re, first_im), (twist_cos[:, None, :], -twist_sin[:, None, :]))
     stacked = jnp.stack(first_pair, axis=1)
-    moved = lax.all_to_all(stacked, "ctx", split_axis=0, concat_axis=3, tiled=True)
+    moved = pairwise_exchange(stacked, "ctx", 0, 3)
     low_pair = (moved[0, 0], moved[0, 1])
     high_pair = (moved[1, 0], moved[1, 1])
     rows_pair = (jnp.stack([low_pair[0], high_pair[0]]), jnp.stack([low_pair[1], high_pair[1]]))

time: 357 us -> 357 us (level)
  waiting for transfers between devices: 57.2 us -> 46.3 us
  starting transfers between devices: 11.4 us -> 19.5 us
    all_to_all x1 -> x0, waiting for transfers between devices: 43.4 us -> none  [shards(): lax.all_to_all(stacked, 'ctx', split_axis=0, concat_axis=3, tiled=True)]
    ppermute x0 -> x7, waiting for transfers between devices: none -> 34.8 us  [pairwise_exchange(): part = lax.ppermute(part, axis, [(d, d ^ mask) for d in range(ways)])]
    ppermute x0 -> x7, starting transfers between devices: none -> 11.7 us  [pairwise_exchange(): part = lax.ppermute(part, axis, [(d, d ^ mask) for d in range(ways)])]
    another operation x4, local copies, waits for them, and re-layouts: 1.46 us -> 7.72 us  [shards(): jnp.stack([low_pair[1], high_pair[1]])]
    all_to_all x2 -> x0, local copies, waits for them, and re-layouts: 4.45 us -> none  [shards(): lax.all_to_all(stacked, 'ctx', split_axis=0, concat_axis=3, tiled=True)]
    another operation x4, local copies, waits for them, and re-layouts: 3.54 us -> 7.75 us  [shards(): jnp.stack([low_pair[0], high_pair[0]])]
    all_to_all x1 -> x0, starting transfers between devices: 3.64 us -> none  [shards(): lax.all_to_all(stacked, 'ctx', split_axis=0, concat_axis=3, tiled=True)]
    unnamed x16 -> x20, local copies, waits for them, and re-layouts: 73.3 us -> 71.7 us
  transfers between devices with their start and end apart: 2 -> 8, of which waited for: 2 -> 4; matrix products, arithmetic and copies ran while one was open for 2% -> 1% of each run, Pallas kernels for 0% -> 0%
where the time goes in v1:
time: 357 us; the launch traced here: 352 us
  local copies, waits for them, and re-layouts  135 us (38%)
  blocking collectives  68.6 us (19%)
  other arithmetic  53 us (15%)
  waiting for transfers between devices  46.3 us (13%)
  matrix products  28.7 us (8%)
  starting transfers between devices  19.5 us (5%)
    unnamed x20, local copies, waits for them, and re-layouts  71.7 us
    all_to_all x1, blocking collectives, shards(): lax.all_to_all(stacked, 'ctx', split_axis=3, concat_axis=0, tiled=True)  51.2 us
    unnamed x1, other arithmetic  38.4 us
    ppermute x7, waiting for transfers between devices, pairwise_exchange(): part = lax.ppermute(part, axis, [(d, d ^ mask) for d in range(ways)])  34.8 us
    dot_general x20, matrix products, contract(): return jnp.einsum(form, left, right, precision=lax.Precision.HIGHEST)  28.7 us
    all_to_all x3, local copies, waits for them, and re-layouts, shards(): lax.all_to_all(stacked, 'ctx', split_axis=3, concat_axis=0, tiled=True)  18.9 us
    all_to_all x1, blocking collectives, shards(): lax.all_to_all(rows_all, 'ctx', split_axis=0, concat_axis=2, tiled=True)  17.4 us
    another operation x1, local copies, waits for them, and re-layouts, shards(): stacked = jnp.stack(turned, axis=1)  15.2 us
  transfers between devices with their start and end apart: 8, of which 4 were waited for; matrix products, arithmetic and copies ran while one was open for 1% of the time, Pallas kernels for 0%

profile of v1, /device:TPU:0, one launch (start us, length us, event | category | flops | bytes accessed | tf_op | source)
XLA Modules:
  0.0 351.6 jit_solution(9312977398790107204)
XLA Ops:
  0.0 3.5 copy.46
  4.0 38.4 %reduce = f32[8192,16]{1,0:T(8,128)} reduce(f32[8192,1,16]{2,1,0:T(1,128)} %bitcast.152, f32[]{:T(128)} %broadcast.483), dimensions={1}, to_apply=%bitcast.134.reduce_sub_computation | reduce | bytes 1048580
  42.4 4.5 %reshape.260 = f32[8,1,16384]{2,1,0:T(1,128)} reshape(f32[8192,16]{1,0:T(8,128)} %reduce) | data formatting | bytes 1048576
  47.0 7.8 %all-to-all-start = ((f32[8,1,16384]{2,1,0:T(1,128)}), f32[8,1,16384]{2,1,0:T(1,128)S(1)}, u32[]{:S(2)}, u32[]{:S(2)}) async-start(f32[8,1,16384]{2,1,0:T(1,128)} %reshape.260), calls=%async_computation | async-start | bytes 1048576 | tf_op jit(solution)/shard_map/all_to_all | solution.py:81
  57.7 11.5 %all-to-all-done = f32[8,1,16384]{2,1,0:T(1,128)S(1)} async-done(((f32[8,1,16384]{2,1,0:T(1,128)}), f32[8,1,16384]{2,1,0:T(1,128)S(1)}, u32[]{:S(2)}, u32[]{:S(2)}) %all-to-all-start) | async-done | bytes 524320 | tf_op jit(solution)/shard_map/all_to_all | solution.py:81
  71.1 10.2 %reshape.261 = f32[8192,1,16]{2,1,0:T(1,128)} reshape(f32[8,16384]{1,0:T(8,128)S(1)} %reduce.1) | data formatting | bytes 1048576
  81.3 3.0 copy.74
  96.6 17.9 %collective-permute-done.1 = f32[2,2,16,1024]{3,0,2,1:T(2,128)S(1)} collective-permute-done((f32[2,2,16,1024]{3,0,2,1:T(2,128)S(1)}, f32[2,2,16,1024]{3,0,2,1:T(2,128)S(1)}, u32[]{:S(2)}, u32[]{:S(2)}) %collective-permute-start.1) | collective-permute-done | bytes 262176 | tf_op jit(solution)/shard_map/ppermute | solution.py:19
  114.5 3.3 collective-permute-start.3
  117.9 3.5 %collective-permute-done.2 = f32[2,2,16,1024]{3,0,2,1:T(2,128)S(1)} collective-permute-done((f32[2,2,16,1024]{3,0,2,1:T(2,128)S(1)}, f32[2,2,16,1024]{3,0,2,1:T(2,128)S(1)}, u32[]{:S(2)}, u32[]{:S(2)}) %collective-permute-start.2) | collective-permute-done | bytes 262176 | tf_op jit(solution)/shard_map/ppermute | solution.py:19
  121.5 13.3 %collective-permute-done.3 = f32[2,2,16,1024]{3,0,2,1:T(2,128)S(1)} collective-permute-done((f32[2,2,16,1024]{3,0,2,1:T(2,128)S(1)}, f32[2,2,16,1024]{3,0,2,1:T(2,128)S(1)}, u32[]{:S(2)}, u32[]{:S(2)}) %collective-permute-start.3) | collective-permute-done | bytes 262176 | tf_op jit(solution)/shard_map/ppermute | solution.py:19
  142.4 2.4 stack.49
  147.2 2.4 stack.47
  169.9 2.6 fusion.13
  177.9 3.4 fusion.1
  186.3 15.2 %copy.63 = f32[2,2,16,8192]{2,0,1,3:T(2,128)} copy(f32[2,2,16,8192]{3,2,0,1:T(8,128)S(1)} %pad_maximum_fusion) | data formatting | bytes 4194304 | tf_op jit(solution)/shard_map/stack | solution.py:107
  201.6 24.0 %reshape.262 = f32[8,1,65536]{2,1,0:T(1,128)S(1)} reshape(f32[8192,2,2,16]{3,2,1,0:T(2,128)} %bitcast.149) | data formatting | bytes 4194304
  225.6 51.2 %all_to_all.51 = f32[8,1,65536]{2,1,0:T(1,128)} all-to-all(f32[8,1,65536]{2,1,0:T(1,128)S(1)} %reshape.262), channel_id=1, replica_groups=mesh['ctx'=8,'ch'=4] {'ctx'}, dimensions={0} | all-to-all | bytes 4194304 | tf_op jit(solution)/shard_map/all_to_all | solution.py:108
  276.9 7.2 %reduce.2 = f32[8,65536]{1,0:T(8,128)S(1)} reduce(f32[8,1,65536]{2,1,0:T(1,128)} %all_to_all.51, f32[]{:T(128)} %broadcast.483), dimensions={1}, to_apply=%all_to_all.41.reduce_sub_computation | reduce | bytes 4194308 | tf_op jit(solution)/shard_map/all_to_all | solution.py:108
  284.1 28.5 %reshape.263 = f32[8192,2,2,16]{3,2,1,0:T(2,128)} reshape(f32[8,65536]{1,0:T(8,128)S(1)} %reduce.2) | data formatting | bytes 4194304
  312.5 13.2 %copy.76 = f32[2,2,16,8,1024]{4,3,2,1,0:T(8,128)S(1)} copy(f32[2,2,16,8,1024]{2,0,1,4,3:T(2,128)} %bitcast.150) | data formatting | bytes 4194304 | tf_op jit(solution)/shard_map/all_to_all | solution.py:108
  325.7 3.0 copy.65
  328.7 2.7 all_to_all.44
  333.0 17.4 %all_to_all.52 = f32[8,16,1024]{2,1,0:T(8,128)S(1)} all-to-all(f32[8,16,1024]{2,1,0:T(8,128)S(1)} %copy.66), channel_id=1, replica_groups=mesh['ctx'=8,'ch'=4] {'ctx'}, dimensions={0} | all-to-all | bytes 1048576 | tf_op jit(solution)/shard_map/all_to_all | solution.py:114
  (82 shorter events, 60.4 us)
Async XLA Ops:
  42.4 13.9 %copy-start.3 = (f32[2,2,16,8192]{3,2,1,0:T(8,128)S(1)}, f32[2,2,16,8192]{3,2,1,0:T(8,128)}, u32[]{:S(2)}) copy-start(f32[2,2,16,8192]{3,2,1,0:T(8,128)} %param.7) | copy-start | bytes 6291460
  47.0 22.2 %all-to-all-start = ((f32[8,1,16384]{2,1,0:T(1,128)}), f32[8,1,16384]{2,1,0:T(1,128)S(1)}, u32[]{:S(2)}, u32[]{:S(2)}) async-start(f32[8,1,16384]{2,1,0:T(1,128)} %reshape.260), calls=%async_computation | async-start | bytes 1048576 | tf_op jit(solution)/shard_map/all_to_all | solution.py:81
  87.6 7.9 %collective-permute-start = (f32[2,2,16,1024]{3,0,2,1:T(2,128)S(1)}, f32[2,2,16,1024]{3,0,2,1:T(2,128)S(1)}, u32[]{:S(2)}, u32[]{:S(2)}) collective-permute-start(f32[2,2,16,1024]{3,0,2,1:T(2,128)S(1)} %get-tuple-element.17), channel_id=1, source_target_pairs={{0,4},{4,0},{8,12},{12,8},{16,20},{20,16},{24,28},{28,24},{1,5},{5... | collective-permute-start | bytes 786440 | tf_op jit(solution)/shard_map/ppermute | solution.py:19
  89.4 45.7 %collective-permute-start.5 = (f32[2,2,16,1024]{3,0,2,1:T(2,128)S(1)}, f32[2,2,16,1024]{3,0,2,1:T(2,128)S(1)}, u32[]{:S(2)}, u32[]{:S(2)}) collective-permute-start(f32[2,2,16,1024]{3,0,2,1:T(2,128)S(1)} %get-tuple-element.21), channel_id=1, source_target_pairs={{0,24},{4,28},{8,16},{12,20},{16,8},{20,12},{24,0},{28,4},{1,25},{... | collective-permute-start | bytes 786440 | tf_op jit(solution)/shard_map/ppermute | solution.py:19
  90.9 44.1 %collective-permute-start.4 = (f32[2,2,16,1024]{3,0,2,1:T(2,128)S(1)}, f32[2,2,16,1024]{3,0,2,1:T(2,128)S(1)}, u32[]{:S(2)}, u32[]{:S(2)}) collective-permute-start(f32[2,2,16,1024]{3,0,2,1:T(2,128)S(1)} %get-tuple-element.22), channel_id=1, source_target_pairs={{0,20},{4,16},{8,28},{12,24},{16,4},{20,0},{24,12},{28,8},{1,21},{... | collective-permute-start | bytes 786440 | tf_op jit(solution)/shard_map/ppermute | solution.py:19
  91.7 43.6 %collective-permute-start.6 = (f32[2,2,16,1024]{3,0,2,1:T(2,128)S(1)}, f32[2,2,16,1024]{3,0,2,1:T(2,128)S(1)}, u32[]{:S(2)}, u32[]{:S(2)}) collective-permute-start(f32[2,2,16,1024]{3,0,2,1:T(2,128)S(1)} %get-tuple-element.15), channel_id=1, source_target_pairs={{0,28},{4,24},{8,20},{12,16},{16,12},{20,8},{24,4},{28,0},{1,29},{... | collective-permute-start | bytes 786440 | tf_op jit(solution)/shard_map/ppermute | solution.py:19
  93.3 21.3 %collective-permute-start.1 = (f32[2,2,16,1024]{3,0,2,1:T(2,128)S(1)}, f32[2,2,16,1024]{3,0,2,1:T(2,128)S(1)}, u32[]{:S(2)}, u32[]{:S(2)}) collective-permute-start(f32[2,2,16,1024]{3,0,2,1:T(2,128)S(1)} %get-tuple-element.18), channel_id=1, source_target_pairs={{0,8},{4,12},{8,0},{12,4},{16,24},{20,28},{24,16},{28,20},{1,9},{5... | collective-permute-start | bytes 786440 | tf_op jit(solution)/shard_map/ppermute | solution.py:19
  95.5 25.9 %collective-permute-start.2 = (f32[2,2,16,1024]{3,0,2,1:T(2,128)S(1)}, f32[2,2,16,1024]{3,0,2,1:T(2,128)S(1)}, u32[]{:S(2)}, u32[]{:S(2)}) collective-permute-start(f32[2,2,16,1024]{3,0,2,1:T(2,128)S(1)} %get-tuple-element.19), channel_id=1, source_target_pairs={{0,12},{4,8},{8,4},{12,0},{16,28},{20,24},{24,20},{28,16},{1,13},{... | collective-permute-start | bytes 786440 | tf_op jit(solution)/shard_map/ppermute | solution.py:19
  114.5 20.4 %collective-permute-start.3 = (f32[2,2,16,1024]{3,0,2,1:T(2,128)S(1)}, f32[2,2,16,1024]{3,0,2,1:T(2,128)S(1)}, u32[]{:S(2)}, u32[]{:S(2)}) collective-permute-start(f32[2,2,16,1024]{3,0,2,1:T(2,128)S(1)} %get-tuple-element.20), channel_id=1, source_target_pairs={{0,16},{4,20},{8,24},{12,28},{16,0},{20,4},{24,8},{28,12},{1,17},{... | collective-permute-start | bytes 786440 | tf_op jit(solution)/shard_map/ppermute | solution.py:19
  152.0 2.3 copy-start.1
  155.6 1.3 copy-start
  332.7 17.8 %copy-start.2 = (f32[16,8192]{1,0:T(8,128)S(1)}, f32[16,8192]{1,0:T(8,128)}, u32[]{:S(2)}) copy-start(f32[16,8192]{1,0:T(8,128)} %param.4) | copy-start | bytes 1572868
  332.7 17.7 %copy-start.4 = (f32[16,8192]{1,0:T(8,128)S(1)}, f32[16,8192]{1,0:T(8,128)}, u32[]{:S(2)}) copy-start(f32[16,8192]{1,0:T(8,128)} %param.5) | copy-start | bytes 1572868
  332.7 17.7 %copy-start.5 = (f32[16]{0:T(128)S(1)}, f32[16]{0:T(128)}, u32[]{:S(2)}) copy-start(f32[16]{0:T(128)} %param.6) | copy-start | bytes 196
